TPU v7x, 32 devices: a whole 2x2x4 slice. The times are simulated.
32 devices in a mesh: ctx: 32 (over z, y, x, core), head: 1.
Axes of the slice: x: 2, y: 2, z: 4, core: 2. Of those that a mesh axis runs over, the one named last changes fastest.
Arguments:
- rotated_queries: bfloat16 [4096, 4096], P('ctx', 'head'), may hold values from -128 to 128
- rotated_keys: bfloat16 [4096, 2048], P('ctx', 'head'), may hold values from -6 to 6
- projected_values: bfloat16 [4096, 2048], P('ctx', 'head'), may hold values from -6 to 6
- doc_ids: int32 [4096], P('ctx'), may hold values from 0 to 15, never falling along the last dimension, each value on 1 to 2048 neighbouring positions
Outputs:
- attended: bfloat16 [4096, 4096], P('ctx', 'head')
Inputs may be any that keep to these rules, and one draw needn't show every extreme that they name: `doc_ids`: document numbers never fall along the sequence; each document has 1 to 2048 tokens, one exactly 2048.
All inputs are finite; a program needn't handle non-finite values.
Results may differ from a plain program's by a relative error of at most 0.006.
Values may be sent and summed in bfloat16 or wider, within the bound.
A program may use at most 64 MiB of HBM per device.

v0:
```python
import jax
import jax.numpy as jnp
from jax import lax
from jax.sharding import PartitionSpec as P

HEAD_SIZE = 128
VISIBLE_KEYS = 1024
PRE_SCALAR = 168


def shifted(value, axis, steps):
    count = lax.axis_size(axis)
    initial, last = (max(0, -steps), min(count, count - steps))
    return lax.ppermute(value, axis, [(source, source + steps) for source in range(initial, last)])


def visible(query_ids, query_pos, key_ids, key_pos):
    return (
        (key_ids[None, :] == query_ids[:, None])
        & (key_pos[None, :] <= query_pos[:, None])
        & (query_pos[:, None] - key_pos[None, :] < VISIBLE_KEYS)
        & (key_pos[None, :] >= 0)
    )


def per_device(rotated_queries, rotated_keys, projected_values, doc_ids):
    rows = rotated_queries.shape[0]
    kv_width = rotated_keys.shape[1]
    kv_heads = kv_width // HEAD_SIZE
    query_group = rotated_queries.shape[1] // kv_width
    span = VISIBLE_KEYS // rows
    scale = PRE_SCALAR ** (-0.5)
    index = lax.axis_index("ctx")
    blocks = [(rotated_keys, projected_values, doc_ids, 0, 0)]
    for back in range(1, span + 1):
        far_keys, far_values, far_ids = shifted(
            (rotated_keys, projected_values, doc_ids), "ctx", back
        )
        blocks.append((far_keys, far_values, far_ids, back, 0))
    count = rotated_queries.shape[0]
    query_rows = rotated_queries.reshape(count, kv_heads, query_group, HEAD_SIZE)
    query_pos = index * rows + 0 + jnp.arange(count, dtype=jnp.int32)
    state = (
        jnp.full((kv_heads, query_group, count), -1e30, jnp.float32),
        jnp.zeros((kv_heads, query_group, count), jnp.float32),
        jnp.zeros((kv_heads, query_group, count, HEAD_SIZE), jnp.float32),
    )
    for key_rows, values, key_ids, back, offset in blocks:
        length = key_rows.shape[0]
        key_pos = (index - back) * rows + offset + jnp.arange(length, dtype=jnp.int32)
        mask = visible(doc_ids, query_pos, key_ids, key_pos)

        def attend(carry, key_rows=key_rows, values=values, mask=mask, length=length):
            best, total, accum = carry
            scores = (
                jnp.einsum(
                    "tgrd,lgd->grtl",
                    query_rows,
                    key_rows.reshape(length, kv_heads, HEAD_SIZE),
                    preferred_element_type=jnp.float32,
                )
                * scale
            )
            masked = jnp.where(mask, scores, jnp.float32(-1e30))
            new_best = jnp.maximum(best, jnp.max(masked, axis=-1))
            fade = jnp.exp(best - new_best)
            weights = jnp.where(mask, jnp.exp(masked - new_best[..., None]), jnp.float32(0.0))
            total = total * fade + jnp.sum(weights, axis=-1)
            accum = accum * fade[..., None] + jnp.einsum(
                "grtl,lgd->grtd",
                weights.astype(jnp.bfloat16),
                values.reshape(length, kv_heads, HEAD_SIZE),
                preferred_element_type=jnp.float32,
            )
            return (new_best, total, accum)

        state = attend(state)
    best, total, accum = state
    out = accum / total[..., None]
    return (
        jnp.transpose(out, (2, 0, 1, 3))
        .reshape(count, kv_heads * query_group * HEAD_SIZE)
        .astype(jnp.bfloat16)
    )


def solution(mesh):
    in_specs = (P("ctx", "head"), P("ctx", "head"), P("ctx", "head"), P("ctx"))
    out_specs = P("ctx", "head")
    return jax.shard_map(
        per_device, mesh=mesh, in_specs=in_specs, out_specs=out_specs, check_vma=False
    )
```

profile of v0, /device:TPU:0, one launch (start us, length us, event | category | flops | bytes accessed | tf_op | source)
XLA Modules:
  0.0 219.5 jit_solution(1916817168309129079)
XLA Ops:
  0.0 2.5 %collective-permute-start = (s32[128]{0:T(128)}, s32[128]{0:T(128)S(1)}, u32[]{:S(2)}, u32[]{:S(2)}) collective-permute-start(s32[128]{0:T(128)} %param.7), channel_id=1, source_target_pairs={{0,1},{1,2},{2,3},{3,4},{4,5},{5,6},{6,7},{7,8},{8,9},{9,10},{10,1... | collective-permute-start | bytes 1544 | tf_op jit(solution)/shard_map/ppermute | solution.py:14
  2.5 5.6 %collective-permute-start.12 = (s32[128]{0:T(128)}, s32[128]{0:T(128)S(1)}, u32[]{:S(2)}, u32[]{:S(2)}) collective-permute-start(s32[128]{0:T(128)} %param.7), channel_id=1, source_target_pairs={{0,5},{1,6},{2,7},{3,8},{4,9},{5,10},{6,11},{7,12},{8,13},{9,14},{... | collective-permute-start | bytes 1544 | tf_op jit(solution)/shard_map/ppermute | solution.py:14
  8.2 2.9 %collective-permute-start.18 = (s32[128]{0:T(128)}, s32[128]{0:T(128)S(1)}, u32[]{:S(2)}, u32[]{:S(2)}) collective-permute-start(s32[128]{0:T(128)} %param.7), channel_id=1, source_target_pairs={{0,7},{1,8},{2,9},{3,10},{4,11},{5,12},{6,13},{7,14},{8,15},{9,16}... | collective-permute-start | bytes 1544 | tf_op jit(solution)/shard_map/ppermute | solution.py:14
  11.1 3.4 %collective-permute-start.3 = (s32[128]{0:T(128)}, s32[128]{0:T(128)S(1)}, u32[]{:S(2)}, u32[]{:S(2)}) collective-permute-start(s32[128]{0:T(128)} %param.7), channel_id=1, source_target_pairs={{0,2},{1,3},{2,4},{3,5},{4,6},{5,7},{6,8},{7,9},{8,10},{9,11},{10,... | collective-permute-start | bytes 1544 | tf_op jit(solution)/shard_map/ppermute | solution.py:14
  14.5 3.4 %collective-permute-start.6 = (s32[128]{0:T(128)}, s32[128]{0:T(128)S(1)}, u32[]{:S(2)}, u32[]{:S(2)}) collective-permute-start(s32[128]{0:T(128)} %param.7), channel_id=1, source_target_pairs={{0,3},{1,4},{2,5},{3,6},{4,7},{5,8},{6,9},{7,10},{8,11},{9,12},{10... | collective-permute-start | bytes 1544 | tf_op jit(solution)/shard_map/ppermute | solution.py:14
  18.2 1.8 reshape.407
  20.0 1.0 copy.38
  21.1 2.1 copy.108
  23.2 4.3 %collective-permute-start.15 = (s32[128]{0:T(128)S(1)}, s32[128]{0:T(128)S(1)}, u32[]{:S(2)}, u32[]{:S(2)}) collective-permute-start(s32[128]{0:T(128)S(1)} %copy-done.22), channel_id=1, source_target_pairs={{0,6},{1,7},{2,8},{3,9},{4,10},{5,11},{6,12},{7,13},{8,14},{9,15},... | collective-permute-start | bytes 1544 | tf_op jit(solution)/shard_map/ppermute | solution.py:14
  27.5 2.3 %collective-permute-start.21 = (s32[128]{0:T(128)S(1)}, s32[128]{0:T(128)S(1)}, u32[]{:S(2)}, u32[]{:S(2)}) collective-permute-start(s32[128]{0:T(128)S(1)} %copy-done.22), channel_id=1, source_target_pairs={{0,8},{1,9},{2,10},{3,11},{4,12},{5,13},{6,14},{7,15},{8,16},{9,17... | collective-permute-start | bytes 1544 | tf_op jit(solution)/shard_map/ppermute | solution.py:14
  29.8 2.4 %collective-permute-start.9 = (s32[128]{0:T(128)S(1)}, s32[128]{0:T(128)S(1)}, u32[]{:S(2)}, u32[]{:S(2)}) collective-permute-start(s32[128]{0:T(128)S(1)} %copy-done.22), channel_id=1, source_target_pairs={{0,4},{1,5},{2,6},{3,7},{4,8},{5,9},{6,10},{7,11},{8,12},{9,13},{1... | collective-permute-start | bytes 1544 | tf_op jit(solution)/shard_map/ppermute | solution.py:14
  32.3 1.7 collective-permute-start.8
  34.0 3.1 %collective-permute-start.7 = (bf16[128,2048]{0,1:T(8,128)(2,1)}, bf16[128,2048]{0,1:T(8,128)(2,1)S(1)}, u32[]{:S(2)}, u32[]{:S(2)}) collective-permute-start(bf16[128,2048]{0,1:T(8,128)(2,1)} %copy.38), channel_id=1, source_target_pairs={{0,3},{1,4},{2,5},{3,6},{4,7},{5,8},{6,9},{7,10},{8,11},{9,12},{10... | collective-permute-start | bytes 1572872 | tf_op jit(solution)/shard_map/ppermute | solution.py:14
  37.1 0.4 fusion.102
  37.5 2.6 %fusion.10 = (f32[16,2,128]{2,1,0:T(2,128)}, f32[16,128,128,2]{2,1,3,0:T(8,128)}) fusion(pred[128,128]{0,1:T(8,128)(4,1)S(1)} %get-tuple-element.26, bf16[128,16,2,128]{3,2,1,0:T(2,128)(2,1)S(1)} %reshape.407, bf16[128,16,128,1]{2,1,0,3:T(8,128)(2,1)S(1)} %bitcast.416), kind=kOutput, calls=%fused_computation.37 | convolution fusion | flops 135786496 | bytes 3702784 | tf_op jit(solution)/shard_map/tgrd,lgd->grtl/dot_general | solution.py:56
  40.1 2.3 %collective-permute-start.1 = (bf16[128,2048]{0,1:T(8,128)(2,1)}, bf16[128,2048]{0,1:T(8,128)(2,1)S(1)}, u32[]{:S(2)}, u32[]{:S(2)}) collective-permute-start(bf16[128,2048]{0,1:T(8,128)(2,1)} %copy.38), channel_id=1, source_target_pairs={{0,1},{1,2},{2,3},{3,4},{4,5},{5,6},{6,7},{7,8},{8,9},{9,10},{10,1... | collective-permute-start | bytes 1572872 | tf_op jit(solution)/shard_map/ppermute | solution.py:14
  42.5 3.3 %collective-permute-start.19 = (bf16[128,2048]{0,1:T(8,128)(2,1)}, bf16[128,2048]{0,1:T(8,128)(2,1)S(1)}, u32[]{:S(2)}, u32[]{:S(2)}) collective-permute-start(bf16[128,2048]{0,1:T(8,128)(2,1)} %copy.38), channel_id=1, source_target_pairs={{0,7},{1,8},{2,9},{3,10},{4,11},{5,12},{6,13},{7,14},{8,15},{9,16}... | collective-permute-start | bytes 1572872 | tf_op jit(solution)/shard_map/ppermute | solution.py:14
  45.8 3.0 %collective-permute-start.13 = (bf16[128,2048]{0,1:T(8,128)(2,1)}, bf16[128,2048]{0,1:T(8,128)(2,1)}, u32[]{:S(2)}, u32[]{:S(2)}) collective-permute-start(bf16[128,2048]{0,1:T(8,128)(2,1)} %copy.38), channel_id=1, source_target_pairs={{0,5},{1,6},{2,7},{3,8},{4,9},{5,10},{6,11},{7,12},{8,13},{9,14},{... | collective-permute-start | bytes 1572872 | tf_op jit(solution)/shard_map/ppermute | solution.py:14
  49.0 3.0 %collective-permute-start.4 = (bf16[128,2048]{0,1:T(8,128)(2,1)}, bf16[128,2048]{0,1:T(8,128)(2,1)}, u32[]{:S(2)}, u32[]{:S(2)}) collective-permute-start(bf16[128,2048]{0,1:T(8,128)(2,1)} %copy.38), channel_id=1, source_target_pairs={{0,2},{1,3},{2,4},{3,5},{4,6},{5,7},{6,8},{7,9},{8,10},{9,11},{10,... | collective-permute-start | bytes 1572872 | tf_op jit(solution)/shard_map/ppermute | solution.py:14
  52.0 1.0 copy.51
  53.0 6.8 %collective-permute-start.22 = (bf16[128,2048]{0,1:T(8,128)(2,1)}, bf16[128,2048]{0,1:T(8,128)(2,1)S(1)}, u32[]{:S(2)}, u32[]{:S(2)}) collective-permute-start(bf16[128,2048]{0,1:T(8,128)(2,1)} %copy.38), channel_id=1, source_target_pairs={{0,8},{1,9},{2,10},{3,11},{4,12},{5,13},{6,14},{7,15},{8,16},{9,17... | collective-permute-start | bytes 1572872 | tf_op jit(solution)/shard_map/ppermute | solution.py:14
  59.9 2.0 fusion.13
  61.8 4.3 %collective-permute-start.16 = (bf16[128,2048]{0,1:T(8,128)(2,1)}, bf16[128,2048]{0,1:T(8,128)(2,1)S(1)}, u32[]{:S(2)}, u32[]{:S(2)}) collective-permute-start(bf16[128,2048]{0,1:T(8,128)(2,1)} %copy.38), channel_id=1, source_target_pairs={{0,6},{1,7},{2,8},{3,9},{4,10},{5,11},{6,12},{7,13},{8,14},{9,15},... | collective-permute-start | bytes 1572872 | tf_op jit(solution)/shard_map/ppermute | solution.py:14
  66.2 2.0 fusion.11
  68.2 24.6 %collective-permute-start.10 = (bf16[128,2048]{0,1:T(8,128)(2,1)}, bf16[128,2048]{0,1:T(8,128)(2,1)S(1)}, u32[]{:S(2)}, u32[]{:S(2)}) collective-permute-start(bf16[128,2048]{0,1:T(8,128)(2,1)} %copy.38), channel_id=1, source_target_pairs={{0,4},{1,5},{2,6},{3,7},{4,8},{5,9},{6,10},{7,11},{8,12},{9,13},{1... | collective-permute-start | bytes 1572872 | tf_op jit(solution)/shard_map/ppermute | solution.py:14
  92.8 1.7 fusion.17
  94.5 2.1 collective-permute-start.14
  96.6 3.1 %fusion.15 = (f32[16,2,128]{2,1,0:T(2,128)S(1)}, f32[16,128,128,2]{2,1,3,0:T(8,128)}) fusion(pred[128,128]{0,1:T(8,128)(4,1)S(1)} %get-tuple-element.28, bf16[128,16,128,1]{0,2,3,1:T(8,128)(2,1)} %bitcast.100, bf16[128,16,2,128]{3,2,1,0:T(2,128)(2,1)S(1)} %reshape.407), kind=kOutput, calls=%fused_computation.42 | convolution fusion | flops 135786496 | bytes 3702784 | tf_op jit(solution)/shard_map/tgrd,lgd->grtl/dot_general | solution.py:56
  99.7 4.0 %collective-permute-start.5 = (bf16[128,2048]{1,0:T(8,128)(2,1)}, bf16[128,2048]{1,0:T(8,128)(2,1)S(1)}, u32[]{:S(2)}, u32[]{:S(2)}) collective-permute-start(bf16[128,2048]{1,0:T(8,128)(2,1)} %param.6), channel_id=1, source_target_pairs={{0,2},{1,3},{2,4},{3,5},{4,6},{5,7},{6,8},{7,9},{8,10},{9,11},{10,... | collective-permute-start | bytes 1572872 | tf_op jit(solution)/shard_map/ppermute | solution.py:14
  103.7 3.0 %fusion.12 = (f32[16,2,128]{2,1,0:T(2,128)S(1)}, f32[16,128,128,2]{2,1,3,0:T(8,128)}) fusion(pred[128,128]{0,1:T(8,128)(4,1)S(1)} %get-tuple-element.29, bf16[128,16,128,1]{0,2,3,1:T(8,128)(2,1)} %bitcast.88, bf16[128,16,2,128]{3,2,1,0:T(2,128)(2,1)S(1)} %reshape.407), kind=kOutput, calls=%fused_computation.39 | convolution fusion | flops 135786496 | bytes 3702784 | tf_op jit(solution)/shard_map/tgrd,lgd->grtl/dot_general | solution.py:56
  106.7 3.2 %collective-permute-start.2 = (bf16[128,2048]{1,0:T(8,128)(2,1)}, bf16[128,2048]{1,0:T(8,128)(2,1)}, u32[]{:S(2)}, u32[]{:S(2)}) collective-permute-start(bf16[128,2048]{1,0:T(8,128)(2,1)} %param.6), channel_id=1, source_target_pairs={{0,1},{1,2},{2,3},{3,4},{4,5},{5,6},{6,7},{7,8},{8,9},{9,10},{10,1... | collective-permute-start | bytes 1572872 | tf_op jit(solution)/shard_map/ppermute | solution.py:14
  109.9 2.0 fusion.18
  111.9 2.3 %collective-permute-start.11 = (bf16[128,2048]{1,0:T(8,128)(2,1)}, bf16[128,2048]{1,0:T(8,128)(2,1)}, u32[]{:S(2)}, u32[]{:S(2)}) collective-permute-start(bf16[128,2048]{1,0:T(8,128)(2,1)} %param.6), channel_id=1, source_target_pairs={{0,4},{1,5},{2,6},{3,7},{4,8},{5,9},{6,10},{7,11},{8,12},{9,13},{1... | collective-permute-start | bytes 1572872 | tf_op jit(solution)/shard_map/ppermute | solution.py:14
  114.1 2.0 fusion.16
  116.1 15.4 %collective-permute-start.17 = (bf16[128,2048]{1,0:T(8,128)(2,1)}, bf16[128,2048]{1,0:T(8,128)(2,1)}, u32[]{:S(2)}, u32[]{:S(2)}) collective-permute-start(bf16[128,2048]{1,0:T(8,128)(2,1)} %param.6), channel_id=1, source_target_pairs={{0,6},{1,7},{2,8},{3,9},{4,10},{5,11},{6,12},{7,13},{8,14},{9,15},... | collective-permute-start | bytes 1572872 | tf_op jit(solution)/shard_map/ppermute | solution.py:14
  131.5 2.0 fusion.14
  133.6 0.8 copy-done.12
  134.4 27.1 %collective-permute-start.20 = (bf16[128,2048]{1,0:T(8,128)(2,1)}, bf16[128,2048]{1,0:T(8,128)(2,1)}, u32[]{:S(2)}, u32[]{:S(2)}) collective-permute-start(bf16[128,2048]{1,0:T(8,128)(2,1)} %param.6), channel_id=1, source_target_pairs={{0,7},{1,8},{2,9},{3,10},{4,11},{5,12},{6,13},{7,14},{8,15},{9,16}... | collective-permute-start | bytes 1572872 | tf_op jit(solution)/shard_map/ppermute | solution.py:14
  161.5 1.3 copy.46
  162.8 3.9 %fusion.46 = f32[16,2,128,128]{2,3,1,0:T(8,128)} fusion(bf16[128,16,128,1]{0,2,3,1:T(8,128)(2,1)} %bitcast.401, f32[16,128,128,2]{2,1,3,0:T(8,128)} %get-tuple-element.46, f32[16,2,128]{2,1,0:T(2,128)S(1)} %get-tuple-element.20, pred[128,128]{0,1:T(8,128)(4,1)S(1)} %get-tuple-element.31), kind=kOutput, calls=%fused_computation.68 | convolution fusion | flops 136839168 | bytes 4751360 | tf_op jit(solution)/shard_map/grtl,lgd->grtd/dot_general | solution.py:69
  166.7 2.0 fusion.48
  168.8 4.8 %collective-permute-start.23 = (bf16[128,2048]{1,0:T(8,128)(2,1)}, bf16[128,2048]{1,0:T(8,128)(2,1)S(1)}, u32[]{:S(2)}, u32[]{:S(2)}) collective-permute-start(bf16[128,2048]{1,0:T(8,128)(2,1)} %param.6), channel_id=1, source_target_pairs={{0,8},{1,9},{2,10},{3,11},{4,12},{5,13},{6,14},{7,15},{8,16},{9,17... | collective-permute-start | bytes 1572872 | tf_op jit(solution)/shard_map/ppermute | solution.py:14
  173.6 1.3 copy.41
  174.9 3.7 %fusion.50 = f32[16,2,128,128]{2,3,1,0:T(8,128)} fusion(bf16[128,16,128,1]{0,2,3,1:T(8,128)(2,1)S(1)} %bitcast.405, f32[16,128,128,2]{2,1,3,0:T(8,128)} %get-tuple-element.50, f32[16,2,128]{2,1,0:T(2,128)S(1)} %get-tuple-element.22, pred[128,128]{0,1:T(8,128)(4,1)S(1)} %get-tuple-element.27), kind=kOutput, calls=%fused_computation.70 | convolution fusion | flops 136839168 | bytes 4751360 | tf_op jit(solution)/shard_map/grtl,lgd->grtd/dot_general | solution.py:69
  178.7 2.0 fusion.52
  180.7 1.9 fusion.19
  182.6 1.3 copy.56
  183.9 3.7 %fusion.44 = f32[16,2,128,128]{2,3,1,0:T(8,128)} fusion(bf16[128,16,128,1]{0,2,3,1:T(8,128)(2,1)S(1)} %bitcast.406, f32[16,128,128,2]{2,1,3,0:T(8,128)} %get-tuple-element.44, f32[16,2,128]{2,1,0:T(2,128)S(1)} %get-tuple-element.19, pred[128,128]{0,1:T(8,128)(4,1)S(1)} %get-tuple-element.32), kind=kOutput, calls=%fused_computation.67 | convolution fusion | flops 136839168 | bytes 4751360 | tf_op jit(solution)/shard_map/grtl,lgd->grtd/dot_general | solution.py:69
  187.7 1.3 fusion.23
  189.0 1.3 copy.66
  190.3 3.7 %fusion.40 = f32[16,2,128,128]{2,3,1,0:T(8,128)} fusion(bf16[128,16,128,1]{0,2,3,1:T(8,128)(2,1)S(1)} %bitcast.407, f32[16,128,128,2]{2,1,3,0:T(8,128)} %get-tuple-element.40, f32[16,2,128]{2,1,0:T(2,128)S(1)} %get-tuple-element.17, pred[128,128]{0,1:T(8,128)(4,1)S(1)} %get-tuple-element.33), kind=kOutput, calls=%fused_computation.65 | convolution fusion | flops 136839168 | bytes 4751360 | tf_op jit(solution)/shard_map/grtl,lgd->grtd/dot_general | solution.py:69
  194.1 0.6 fusion.35
  194.6 1.0 copy-done.6
  195.6 1.3 fusion.27
  197.0 1.3 copy.61
  198.3 3.7 %fusion.42 = f32[16,2,128,128]{2,3,1,0:T(8,128)} fusion(bf16[128,16,128,1]{0,2,3,1:T(8,128)(2,1)S(1)} %bitcast.408, f32[16,128,128,2]{2,1,3,0:T(8,128)} %get-tuple-element.42, f32[16,2,128]{2,1,0:T(2,128)S(1)} %get-tuple-element.18, pred[128,128]{0,1:T(8,128)(4,1)S(1)} %get-tuple-element.28), kind=kOutput, calls=%fused_computation.66 | convolution fusion | flops 136839168 | bytes 4751360 | tf_op jit(solution)/shard_map/grtl,lgd->grtd/dot_general | solution.py:69
  202.1 0.6 bitcast_maximum_fusion.3
  202.7 1.9 fusion.29
  204.6 1.3 copy.71
  206.0 1.5 bitcast_add_fusion.9
  207.5 2.0 fusion.38
  209.5 0.3 copy.76
  209.8 8.4 %fusion.1 = bf16[128,16,2,128]{0,3,2,1:T(8,128)(2,1)S(1)} fusion(f32[16,2,128,128]{2,3,1,0:T(8,128)} %fusion.38, f32[16,2,128,128]{2,3,1,0:T(8,128)} %fusion.40, f32[16,2,128,128]{2,3,1,0:T(8,128)} %fusion.42, f32[16,2,128,128]{2,3,1,0:T(8,128)} %fusion.44, f32[16,2,128,128]{2,3,1,0:T(8,128)} %fusion.46, f32[16,2,128,128]{2,3,1,0:T(8,128)} %fusion.48, ...), kind=kOutput, calls=%fused_computation.2 | convolution fusion | flops 146800640 | bytes 20643840 | tf_op jit(solution)/shard_map/grtl,lgd->grtd/dot_general | solution.py:69
  218.2 1.3 copy.78
  (89 shorter events, 0.6 us)
Async XLA Ops:
  0.0 20.0 %copy-start.10 = (bf16[128,2048]{1,0:T(8,128)(2,1)S(1)}, bf16[128,2048]{1,0:T(8,128)(2,1)}, u32[]{:S(2)}) copy-start(bf16[128,2048]{1,0:T(8,128)(2,1)} %param.5) | copy-start | bytes 1572868
  0.0 23.2 %collective-permute-start = (s32[128]{0:T(128)}, s32[128]{0:T(128)S(1)}, u32[]{:S(2)}, u32[]{:S(2)}) collective-permute-start(s32[128]{0:T(128)} %param.7), channel_id=1, source_target_pairs={{0,1},{1,2},{2,3},{3,4},{4,5},{5,6},{6,7},{7,8},{8,9},{9,10},{10,1... | collective-permute-start | bytes 1544 | tf_op jit(solution)/shard_map/ppermute | solution.py:14
  2.5 25.0 %collective-permute-start.12 = (s32[128]{0:T(128)}, s32[128]{0:T(128)S(1)}, u32[]{:S(2)}, u32[]{:S(2)}) collective-permute-start(s32[128]{0:T(128)} %param.7), channel_id=1, source_target_pairs={{0,5},{1,6},{2,7},{3,8},{4,9},{5,10},{6,11},{7,12},{8,13},{9,14},{... | collective-permute-start | bytes 1544 | tf_op jit(solution)/shard_map/ppermute | solution.py:14
  8.2 21.7 %collective-permute-start.18 = (s32[128]{0:T(128)}, s32[128]{0:T(128)S(1)}, u32[]{:S(2)}, u32[]{:S(2)}) collective-permute-start(s32[128]{0:T(128)} %param.7), channel_id=1, source_target_pairs={{0,7},{1,8},{2,9},{3,10},{4,11},{5,12},{6,13},{7,14},{8,15},{9,16}... | collective-permute-start | bytes 1544 | tf_op jit(solution)/shard_map/ppermute | solution.py:14
  11.1 21.2 %collective-permute-start.3 = (s32[128]{0:T(128)}, s32[128]{0:T(128)S(1)}, u32[]{:S(2)}, u32[]{:S(2)}) collective-permute-start(s32[128]{0:T(128)} %param.7), channel_id=1, source_target_pairs={{0,2},{1,3},{2,4},{3,5},{4,6},{5,7},{6,8},{7,9},{8,10},{9,11},{10,... | collective-permute-start | bytes 1544 | tf_op jit(solution)/shard_map/ppermute | solution.py:14
  14.5 19.5 %collective-permute-start.6 = (s32[128]{0:T(128)}, s32[128]{0:T(128)S(1)}, u32[]{:S(2)}, u32[]{:S(2)}) collective-permute-start(s32[128]{0:T(128)} %param.7), channel_id=1, source_target_pairs={{0,3},{1,4},{2,5},{3,6},{4,7},{5,8},{6,9},{7,10},{8,11},{9,12},{10... | collective-permute-start | bytes 1544 | tf_op jit(solution)/shard_map/ppermute | solution.py:14
  20.0 3.2 %copy-start.22 = (s32[128]{0:T(128)S(1)}, s32[128]{0:T(128)}, u32[]{:S(2)}) copy-start(s32[128]{0:T(128)} %param.7) | copy-start | bytes 1540
  23.2 17.0 %collective-permute-start.15 = (s32[128]{0:T(128)S(1)}, s32[128]{0:T(128)S(1)}, u32[]{:S(2)}, u32[]{:S(2)}) collective-permute-start(s32[128]{0:T(128)S(1)} %copy-done.22), channel_id=1, source_target_pairs={{0,6},{1,7},{2,8},{3,9},{4,10},{5,11},{6,12},{7,13},{8,14},{9,15},... | collective-permute-start | bytes 1544 | tf_op jit(solution)/shard_map/ppermute | solution.py:14
  27.5 14.9 %collective-permute-start.21 = (s32[128]{0:T(128)S(1)}, s32[128]{0:T(128)S(1)}, u32[]{:S(2)}, u32[]{:S(2)}) collective-permute-start(s32[128]{0:T(128)S(1)} %copy-done.22), channel_id=1, source_target_pairs={{0,8},{1,9},{2,10},{3,11},{4,12},{5,13},{6,14},{7,15},{8,16},{9,17... | collective-permute-start | bytes 1544 | tf_op jit(solution)/shard_map/ppermute | solution.py:14
  29.8 15.9 %collective-permute-start.9 = (s32[128]{0:T(128)S(1)}, s32[128]{0:T(128)S(1)}, u32[]{:S(2)}, u32[]{:S(2)}) collective-permute-start(s32[128]{0:T(128)S(1)} %copy-done.22), channel_id=1, source_target_pairs={{0,4},{1,5},{2,6},{3,7},{4,8},{5,9},{6,10},{7,11},{8,12},{9,13},{1... | collective-permute-start | bytes 1544 | tf_op jit(solution)/shard_map/ppermute | solution.py:14
  32.3 16.7 %collective-permute-start.8 = (bf16[128,2048]{1,0:T(8,128)(2,1)}, bf16[128,2048]{1,0:T(8,128)(2,1)S(1)}, u32[]{:S(2)}, u32[]{:S(2)}) collective-permute-start(bf16[128,2048]{1,0:T(8,128)(2,1)} %param.6), channel_id=1, source_target_pairs={{0,3},{1,4},{2,5},{3,6},{4,7},{5,8},{6,9},{7,10},{8,11},{9,12},{10... | collective-permute-start | bytes 1572872 | tf_op jit(solution)/shard_map/ppermute | solution.py:14
  34.0 19.0 %collective-permute-start.7 = (bf16[128,2048]{0,1:T(8,128)(2,1)}, bf16[128,2048]{0,1:T(8,128)(2,1)S(1)}, u32[]{:S(2)}, u32[]{:S(2)}) collective-permute-start(bf16[128,2048]{0,1:T(8,128)(2,1)} %copy.38), channel_id=1, source_target_pairs={{0,3},{1,4},{2,5},{3,6},{4,7},{5,8},{6,9},{7,10},{8,11},{9,12},{10... | collective-permute-start | bytes 1572872 | tf_op jit(solution)/shard_map/ppermute | solution.py:14
  40.1 21.7 %collective-permute-start.1 = (bf16[128,2048]{0,1:T(8,128)(2,1)}, bf16[128,2048]{0,1:T(8,128)(2,1)S(1)}, u32[]{:S(2)}, u32[]{:S(2)}) collective-permute-start(bf16[128,2048]{0,1:T(8,128)(2,1)} %copy.38), channel_id=1, source_target_pairs={{0,1},{1,2},{2,3},{3,4},{4,5},{5,6},{6,7},{7,8},{8,9},{9,10},{10,1... | collective-permute-start | bytes 1572872 | tf_op jit(solution)/shard_map/ppermute | solution.py:14
  42.5 25.7 %collective-permute-start.19 = (bf16[128,2048]{0,1:T(8,128)(2,1)}, bf16[128,2048]{0,1:T(8,128)(2,1)S(1)}, u32[]{:S(2)}, u32[]{:S(2)}) collective-permute-start(bf16[128,2048]{0,1:T(8,128)(2,1)} %copy.38), channel_id=1, source_target_pairs={{0,7},{1,8},{2,9},{3,10},{4,11},{5,12},{6,13},{7,14},{8,15},{9,16}... | collective-permute-start | bytes 1572872 | tf_op jit(solution)/shard_map/ppermute | solution.py:14
  45.8 48.7 %collective-permute-start.13 = (bf16[128,2048]{0,1:T(8,128)(2,1)}, bf16[128,2048]{0,1:T(8,128)(2,1)}, u32[]{:S(2)}, u32[]{:S(2)}) collective-permute-start(bf16[128,2048]{0,1:T(8,128)(2,1)} %copy.38), channel_id=1, source_target_pairs={{0,5},{1,6},{2,7},{3,8},{4,9},{5,10},{6,11},{7,12},{8,13},{9,14},{... | collective-permute-start | bytes 1572872 | tf_op jit(solution)/shard_map/ppermute | solution.py:14
  49.0 50.7 %collective-permute-start.4 = (bf16[128,2048]{0,1:T(8,128)(2,1)}, bf16[128,2048]{0,1:T(8,128)(2,1)}, u32[]{:S(2)}, u32[]{:S(2)}) collective-permute-start(bf16[128,2048]{0,1:T(8,128)(2,1)} %copy.38), channel_id=1, source_target_pairs={{0,2},{1,3},{2,4},{3,5},{4,6},{5,7},{6,8},{7,9},{8,10},{9,11},{10,... | collective-permute-start | bytes 1572872 | tf_op jit(solution)/shard_map/ppermute | solution.py:14
  53.0 53.7 %collective-permute-start.22 = (bf16[128,2048]{0,1:T(8,128)(2,1)}, bf16[128,2048]{0,1:T(8,128)(2,1)S(1)}, u32[]{:S(2)}, u32[]{:S(2)}) collective-permute-start(bf16[128,2048]{0,1:T(8,128)(2,1)} %copy.38), channel_id=1, source_target_pairs={{0,8},{1,9},{2,10},{3,11},{4,12},{5,13},{6,14},{7,15},{8,16},{9,17... | collective-permute-start | bytes 1572872 | tf_op jit(solution)/shard_map/ppermute | solution.py:14
  61.8 50.0 %collective-permute-start.16 = (bf16[128,2048]{0,1:T(8,128)(2,1)}, bf16[128,2048]{0,1:T(8,128)(2,1)S(1)}, u32[]{:S(2)}, u32[]{:S(2)}) collective-permute-start(bf16[128,2048]{0,1:T(8,128)(2,1)} %copy.38), channel_id=1, source_target_pairs={{0,6},{1,7},{2,8},{3,9},{4,10},{5,11},{6,12},{7,13},{8,14},{9,15},... | collective-permute-start | bytes 1572872 | tf_op jit(solution)/shard_map/ppermute | solution.py:14
  68.2 24.6 %copy-start.11 = (bf16[128,2048]{0,1:T(8,128)(2,1)}, bf16[128,2048]{0,1:T(8,128)(2,1)S(1)}, u32[]{:S(2)}) copy-start(bf16[128,2048]{0,1:T(8,128)(2,1)S(1)} %collective-permute-done.19) | copy-start | bytes 1572868
  68.2 48.0 %collective-permute-start.10 = (bf16[128,2048]{0,1:T(8,128)(2,1)}, bf16[128,2048]{0,1:T(8,128)(2,1)S(1)}, u32[]{:S(2)}, u32[]{:S(2)}) collective-permute-start(bf16[128,2048]{0,1:T(8,128)(2,1)} %copy.38), channel_id=1, source_target_pairs={{0,4},{1,5},{2,6},{3,7},{4,8},{5,9},{6,10},{7,11},{8,12},{9,13},{1... | collective-permute-start | bytes 1572872 | tf_op jit(solution)/shard_map/ppermute | solution.py:14
  94.5 102.5 %collective-permute-start.14 = (bf16[128,2048]{1,0:T(8,128)(2,1)}, bf16[128,2048]{1,0:T(8,128)(2,1)}, u32[]{:S(2)}, u32[]{:S(2)}) collective-permute-start(bf16[128,2048]{1,0:T(8,128)(2,1)} %param.6), channel_id=1, source_target_pairs={{0,5},{1,6},{2,7},{3,8},{4,9},{5,10},{6,11},{7,12},{8,13},{9,14},{... | collective-permute-start | bytes 1572872 | tf_op jit(solution)/shard_map/ppermute | solution.py:14
  99.7 33.9 %collective-permute-start.5 = (bf16[128,2048]{1,0:T(8,128)(2,1)}, bf16[128,2048]{1,0:T(8,128)(2,1)S(1)}, u32[]{:S(2)}, u32[]{:S(2)}) collective-permute-start(bf16[128,2048]{1,0:T(8,128)(2,1)} %param.6), channel_id=1, source_target_pairs={{0,2},{1,3},{2,4},{3,5},{4,6},{5,7},{6,8},{7,9},{8,10},{9,11},{10,... | collective-permute-start | bytes 1572872 | tf_op jit(solution)/shard_map/ppermute | solution.py:14
  106.7 62.1 %collective-permute-start.2 = (bf16[128,2048]{1,0:T(8,128)(2,1)}, bf16[128,2048]{1,0:T(8,128)(2,1)}, u32[]{:S(2)}, u32[]{:S(2)}) collective-permute-start(bf16[128,2048]{1,0:T(8,128)(2,1)} %param.6), channel_id=1, source_target_pairs={{0,1},{1,2},{2,3},{3,4},{4,5},{5,6},{6,7},{7,8},{8,9},{9,10},{10,1... | collective-permute-start | bytes 1572872 | tf_op jit(solution)/shard_map/ppermute | solution.py:14
  111.9 70.7 %collective-permute-start.11 = (bf16[128,2048]{1,0:T(8,128)(2,1)}, bf16[128,2048]{1,0:T(8,128)(2,1)}, u32[]{:S(2)}, u32[]{:S(2)}) collective-permute-start(bf16[128,2048]{1,0:T(8,128)(2,1)} %param.6), channel_id=1, source_target_pairs={{0,4},{1,5},{2,6},{3,7},{4,8},{5,9},{6,10},{7,11},{8,12},{9,13},{1... | collective-permute-start | bytes 1572872 | tf_op jit(solution)/shard_map/ppermute | solution.py:14
  116.1 17.5 %copy-start.13 = (f32[16,2,128]{2,1,0:T(2,128)}, f32[16,2,128]{2,1,0:T(2,128)S(1)}, u32[]{:S(2)}) copy-start(f32[16,2,128]{2,1,0:T(2,128)S(1)} %get-tuple-element.39) | copy-start | bytes 49156
  116.1 17.4 %copy-start.15 = (f32[16,2,128]{2,1,0:T(2,128)S(1)}, f32[16,2,128]{2,1,0:T(2,128)}, u32[]{:S(2)}) copy-start(f32[16,2,128]{2,1,0:T(2,128)} %get-tuple-element.51) | copy-start | bytes 49156
  116.1 72.9 %collective-permute-start.17 = (bf16[128,2048]{1,0:T(8,128)(2,1)}, bf16[128,2048]{1,0:T(8,128)(2,1)}, u32[]{:S(2)}, u32[]{:S(2)}) collective-permute-start(bf16[128,2048]{1,0:T(8,128)(2,1)} %param.6), channel_id=1, source_target_pairs={{0,6},{1,7},{2,8},{3,9},{4,10},{5,11},{6,12},{7,13},{8,14},{9,15},... | collective-permute-start | bytes 1572872 | tf_op jit(solution)/shard_map/ppermute | solution.py:14
  133.6 0.8 copy-start.12
  134.4 70.2 %collective-permute-start.20 = (bf16[128,2048]{1,0:T(8,128)(2,1)}, bf16[128,2048]{1,0:T(8,128)(2,1)}, u32[]{:S(2)}, u32[]{:S(2)}) collective-permute-start(bf16[128,2048]{1,0:T(8,128)(2,1)} %param.6), channel_id=1, source_target_pairs={{0,7},{1,8},{2,9},{3,10},{4,11},{5,12},{6,13},{7,14},{8,15},{9,16}... | collective-permute-start | bytes 1572872 | tf_op jit(solution)/shard_map/ppermute | solution.py:14
  162.8 3.9 %copy-start.4 = (f32[16,128,128,2]{2,1,3,0:T(8,128)S(1)}, f32[16,128,128,2]{2,1,3,0:T(8,128)}, u32[]{:S(2)}) copy-start(f32[16,128,128,2]{2,1,3,0:T(8,128)} %get-tuple-element.48) | copy-start | bytes 6291460
  168.8 40.8 %collective-permute-start.23 = (bf16[128,2048]{1,0:T(8,128)(2,1)}, bf16[128,2048]{1,0:T(8,128)(2,1)S(1)}, u32[]{:S(2)}, u32[]{:S(2)}) collective-permute-start(bf16[128,2048]{1,0:T(8,128)(2,1)} %param.6), channel_id=1, source_target_pairs={{0,8},{1,9},{2,10},{3,11},{4,12},{5,13},{6,14},{7,15},{8,16},{9,17... | collective-permute-start | bytes 1572872 | tf_op jit(solution)/shard_map/ppermute | solution.py:14
  174.9 3.8 %copy-start.8 = (f32[16,128,128,2]{2,1,3,0:T(8,128)S(1)}, f32[16,128,128,2]{2,1,3,0:T(8,128)}, u32[]{:S(2)}) copy-start(f32[16,128,128,2]{2,1,3,0:T(8,128)} %get-tuple-element.52) | copy-start | bytes 6291460
  174.9 3.8 %copy-start.9 = (bf16[128,2048]{0,1:T(8,128)(2,1)S(1)}, bf16[128,2048]{0,1:T(8,128)(2,1)}, u32[]{:S(2)}) copy-start(bf16[128,2048]{0,1:T(8,128)(2,1)} %copy.108) | copy-start | bytes 1572868
  178.6 2.0 copy-start.3
  183.9 3.7 %copy-start.2 = (f32[16,128,128,2]{2,1,3,0:T(8,128)S(1)}, f32[16,128,128,2]{2,1,3,0:T(8,128)}, u32[]{:S(2)}) copy-start(f32[16,128,128,2]{2,1,3,0:T(8,128)} %get-tuple-element.46) | copy-start | bytes 6291460
  183.9 3.7 %copy-start.5 = (f32[16,128,128,2]{2,1,3,0:T(8,128)S(1)}, f32[16,128,128,2]{2,1,3,0:T(8,128)}, u32[]{:S(2)}) copy-start(f32[16,128,128,2]{2,1,3,0:T(8,128)} %get-tuple-element.48) | copy-start | bytes 6291460
  190.3 3.7 %copy-start = (f32[16,128,128,2]{2,1,3,0:T(8,128)S(1)}, f32[16,128,128,2]{2,1,3,0:T(8,128)}, u32[]{:S(2)}) copy-start(f32[16,128,128,2]{2,1,3,0:T(8,128)} %get-tuple-element.36) | copy-start | bytes 6291460
  190.3 4.3 %copy-start.7 = (f32[16,128,128,2]{2,1,3,0:T(8,128)S(1)}, f32[16,128,128,2]{2,1,3,0:T(8,128)}, u32[]{:S(2)}) copy-start(f32[16,128,128,2]{2,1,3,0:T(8,128)} %get-tuple-element.44) | copy-start | bytes 6291460
  194.1 1.6 copy-start.6
  198.3 3.8 %copy-start.16 = (f32[16,2,128]{2,1,0:T(2,128)S(1)}, f32[16,2,128]{2,1,0:T(2,128)}, u32[]{:S(2)}) copy-start(f32[16,2,128]{2,1,0:T(2,128)} %get-tuple-element.51) | copy-start | bytes 49156
  198.3 4.4 %copy-start.1 = (f32[16,128,128,2]{2,1,3,0:T(8,128)S(1)}, f32[16,128,128,2]{2,1,3,0:T(8,128)}, u32[]{:S(2)}) copy-start(f32[16,128,128,2]{2,1,3,0:T(8,128)} %get-tuple-element.42) | copy-start | bytes 6291460
  202.7 3.2 %copy-start.14 = (f32[16,2,128]{2,1,0:T(2,128)S(1)}, f32[16,2,128]{2,1,0:T(2,128)}, u32[]{:S(2)}) copy-start(f32[16,2,128]{2,1,0:T(2,128)} %copy-done.13) | copy-start | bytes 49156
  202.7 3.2 %copy-start.17 = (f32[16,2,128]{2,1,0:T(2,128)S(1)}, f32[16,2,128]{2,1,0:T(2,128)}, u32[]{:S(2)}) copy-start(f32[16,2,128]{2,1,0:T(2,128)} %get-tuple-element.53) | copy-start | bytes 49156
  202.7 3.2 %copy-start.18 = (f32[16,2,128]{2,1,0:T(2,128)S(1)}, f32[16,2,128]{2,1,0:T(2,128)}, u32[]{:S(2)}) copy-start(f32[16,2,128]{2,1,0:T(2,128)} %get-tuple-element.54) | copy-start | bytes 49156
  207.5 2.3 %copy-start.19 = (f32[128,16,2]{0,2,1:T(2,128)S(1)}, f32[128,16,2]{0,2,1:T(2,128)}, u32[]{:S(2)}) copy-start(f32[128,16,2]{0,2,1:T(2,128)} %get-tuple-element.10) | copy-start | bytes 49156
  207.5 2.3 %copy-start.20 = (f32[128,16,2]{0,2,1:T(2,128)S(1)}, f32[128,16,2]{0,2,1:T(2,128)}, u32[]{:S(2)}) copy-start(f32[128,16,2]{0,2,1:T(2,128)} %get-tuple-element.11) | copy-start | bytes 49156
  207.5 2.3 %copy-start.21 = (f32[128,16,2]{0,2,1:T(2,128)S(1)}, f32[128,16,2]{0,2,1:T(2,128)}, u32[]{:S(2)}) copy-start(f32[128,16,2]{0,2,1:T(2,128)} %get-tuple-element.12) | copy-start | bytes 49156
where the time goes:
time: 223 us; the launch traced here: 220 us
  starting transfers between devices  138 us (62%)
  matrix products  53.6 us (24%)
  local copies, waits for them, and re-layouts  17.3 us (8%)
  other arithmetic  9.95 us (4%)
    ppermute x24, starting transfers between devices, shifted(): lax.ppermute(value, axis, [(source, source + steps) for source in range(i...  138 us
    dot_general x9, matrix products, attend(): jnp.einsum('grtl,lgd->grtd', weights.astype(jnp.bfloat16), values.reshape...  33.3 us
    dot_general x9, matrix products, attend(): jnp.einsum('tgrd,lgd->grtl', query_rows, key_rows.reshape(length, kv_head...  20.4 us
    ppermute x8, local copies, waits for them, and re-layouts, shifted(): lax.ppermute(value, axis, [(source, source + steps) for source in range(i...  9.13 us
    reduce_sum x5, other arithmetic, attend(): total = total * fade + jnp.sum(weights, axis=-1)  7.05 us
  transfers between devices with their start and end apart: 24, of which 0 were waited for; matrix products, arithmetic and copies ran while one was open for 31% of the time, Pallas kernels for 0%

commit v1 on v0

v1 whole, which is shorter than its diff:
```python
import functools
import math

import jax
import jax.numpy as jnp
from jax import lax
from jax.experimental import pallas as pl
from jax.experimental.pallas import tpu as pltpu
from jax.sharding import PartitionSpec as P

HEAD_SIZE = 128
VISIBLE_KEYS = 1024
PRE_SCALAR = 168
CHUNK_HEADS = 2
MESH = pl.DeviceIdType.MESH


def kernel(
    n,
    group,
    q_hbm,
    k_hbm,
    v_hbm,
    ids_hbm,
    o_hbm,
    kv,
    ids,
    q_buf,
    o_buf,
    bias,
    send_sem,
    recv_sem,
    ids_send_sem,
    ids_recv_sem,
    own_sem,
    q_sem,
    ids_sem,
    out_sem,
):
    rows = q_hbm.shape[0]
    width = k_hbm.shape[1]
    span = VISIBLE_KEYS // rows
    keys = VISIBLE_KEYS + rows
    chips = span // 2
    cols = CHUNK_HEADS * HEAD_SIZE
    chunks = width // cols
    q_cols = cols * group
    direct = chips
    me = lax.axis_index("ctx")
    local = lax.rem(me, span)
    base = me - local
    chip = local // 2
    core = lax.rem(local, 2)
    sib = 2 * chip + 1 - core
    z_next = lax.rem(me + span, n)
    z_prev = lax.rem(me + n - span, n)

    def back(dst, src):
        return lax.rem(dst - src + span, span)

    def place(steps):
        return pl.multiple_of((span - steps) * rows, rows)

    def block(steps, chunk):
        start = pl.multiple_of(chunk * cols, cols)
        return kv.at[:, pl.ds(place(steps), rows), pl.ds(start, cols)]

    def copy(src, dst, target, kind, chunk):
        return pltpu.make_async_remote_copy(
            src_ref=block(src, chunk),
            dst_ref=block(dst, chunk),
            send_sem=send_sem.at[kind, chunk],
            recv_sem=recv_sem.at[dst, chunk],
            device_id={"ctx": target},
            device_id_type=MESH,
        )

    def ids_copy(src, dst, target, kind, chunk):
        return pltpu.make_async_remote_copy(
            src_ref=ids.at[src],
            dst_ref=ids.at[dst],
            send_sem=ids_send_sem.at[kind],
            recv_sem=ids_recv_sem.at[dst],
            device_id={"ctx": target},
            device_id_type=MESH,
        )

    def other(turn):
        return lax.rem(chip + turn, chips)

    def send_own(copy, chunk):
        copy(0, span, z_next, 0, chunk).start()
        for turn in range(1, chips):
            to = 2 * other(turn) + core

            @pl.when(to > local)
            def _():
                copy(0, back(to, local), base + to, turn, chunk).start()

        @pl.when(core == 0)
        def _():
            copy(0, back(sib, local), base + sib, direct, chunk).start()

    def send_past(copy, chunk):
        copy(0, span, z_next, 0, chunk).wait_recv()
        for turn in range(1, chips):
            to = 2 * other(turn) + core

            @pl.when(to < local)
            def _():
                copy(span, back(to, local), base + to, turn, chunk).start()

        @pl.when(core == 1)
        def _():
            copy(span, back(sib, local), base + sib, direct, chunk).start()

    def relay(copy, chunk):
        for turn in range(1, chips):
            source = 2 * other(turn) + core
            here = back(local, source)
            copy(0, here, z_next, 0, chunk).wait_recv()
            copy(here, back(sib, source), base + sib, direct + turn, chunk).start()

    def gather(copy, chunk):
        copy(0, back(local, sib), z_next, 0, chunk).wait_recv()
        for turn in range(1, chips):
            source = 2 * other(turn) + 1 - core
            copy(0, back(local, source), z_next, 0, chunk).wait_recv()

    def own_copies(chunk):
        start = pl.multiple_of(chunk * cols, cols)
        return [
            pltpu.make_async_copy(
                ref.at[:, pl.ds(start, cols)],
                kv.at[which, pl.ds(VISIBLE_KEYS, rows), pl.ds(start, cols)],
                own_sem.at[which, chunk],
            )
            for which, ref in enumerate((k_hbm, v_hbm))
        ]

    q_copy = pltpu.make_async_copy(q_hbm, q_buf, q_sem)
    own_ids = pltpu.make_async_copy(ids_hbm, ids.at[0], ids_sem)

    def out_copy(chunk):
        part = pl.ds(pl.multiple_of(chunk * q_cols, q_cols), q_cols)
        return pltpu.make_async_copy(o_buf.at[:, part], o_hbm.at[:, part], out_sem.at[chunk])

    own_ids.start()

    def fetch(chunk, _):
        for c in own_copies(chunk):
            c.start()
        return 0

    lax.fori_loop(0, chunks, fetch, 0)
    q_copy.start()

    barrier = pltpu.get_barrier_semaphore()
    partners = [z_next, z_prev, base + sib] + [
        base + 2 * other(turn) + core for turn in range(1, chips)
    ]
    for partner in partners:
        pl.semaphore_signal(barrier, inc=1, device_id={"ctx": partner}, device_id_type=MESH)
    pl.semaphore_wait(barrier, len(partners))

    own_ids.wait()
    send_own(ids_copy, 0)

    def start_own(chunk, _):
        for c in own_copies(chunk):
            c.wait()
        send_own(copy, chunk)
        return 0

    lax.fori_loop(0, chunks, start_own, 0)

    send_past(ids_copy, 0)
    send_past(copy, 0)
    relay(ids_copy, 0)
    send_past(copy, 1)
    relay(copy, 0)
    gather(ids_copy, 0)

    own_row = ids[0].astype(jnp.float32)
    query_ids = jnp.broadcast_to(own_row, (rows, rows)).T
    row = lax.broadcasted_iota(jnp.int32, (rows, rows), 0)
    column = lax.broadcasted_iota(jnp.int32, (rows, rows), 1)
    for steps in range(span, -1, -1):
        seen = query_ids == ids[steps].astype(jnp.float32)
        key_pos = (me - steps) * rows + column
        query_pos = me * rows + row
        seen = seen & (key_pos >= 0) & (key_pos <= query_pos)
        seen = seen & (query_pos - key_pos < VISIBLE_KEYS)
        bias[:, (span - steps) * rows : (span - steps + 1) * rows] = jnp.where(
            seen, jnp.float32(0.0), jnp.float32(-1e30)
        )
    q_copy.wait()
    factor = PRE_SCALAR ** (-0.5) * math.log2(math.e)

    def step(chunk, _):
        @pl.when(chunk + 2 < chunks)
        def _():
            send_past(copy, chunk + 2)

        @pl.when(chunk + 1 < chunks)
        def _():
            relay(copy, chunk + 1)

        gather(copy, chunk)
        for head in range(CHUNK_HEADS):
            at = pl.multiple_of(chunk * cols + head * HEAD_SIZE, HEAD_SIZE)
            key_rows = kv[0, :, pl.ds(at, HEAD_SIZE)]
            values = kv[1, :, pl.ds(at, HEAD_SIZE)]
            weights, totals = [], []
            queries = jnp.concatenate(
                [
                    q_buf[:, pl.ds(pl.multiple_of(at * group + g * HEAD_SIZE, HEAD_SIZE), HEAD_SIZE)]
                    for g in range(group)
                ],
                axis=0,
            )
            scores = lax.dot_general(
                queries, key_rows, (((1,), (1,)), ((), ())), preferred_element_type=jnp.float32
            )
            for g in range(group):
                masked = scores[g * rows : (g + 1) * rows] + bias[...]
                top = jnp.max(masked, axis=1, keepdims=True)
                weight = jnp.exp2((masked - top) * factor)
                totals.append(jnp.sum(weight, axis=1, keepdims=True))
                weights.append(weight.astype(jnp.bfloat16))
            summed = jnp.dot(
                jnp.concatenate(weights, axis=0), values, preferred_element_type=jnp.float32
            )
            for g in range(group):
                to = pl.multiple_of(at * group + g * HEAD_SIZE, HEAD_SIZE)
                o_buf[:, pl.ds(to, HEAD_SIZE)] = (
                    summed[g * rows : (g + 1) * rows] / totals[g]
                ).astype(jnp.bfloat16)
        out_copy(chunk).start()
        return 0

    lax.fori_loop(0, chunks, step, 0)

    def finish(chunk, _):
        for kind in range(2 * chips):
            copy(0, span, z_next, kind, chunk).wait_send()
        out_copy(chunk).wait()
        return 0

    lax.fori_loop(0, chunks, finish, 0)
    for kind in range(2 * chips):
        ids_copy(0, span, z_next, kind, 0).wait_send()


def per_device(n, rotated_queries, rotated_keys, projected_values, doc_ids):
    rows, q_width = rotated_queries.shape
    width = rotated_keys.shape[1]
    span = VISIBLE_KEYS // rows
    chunks = width // (CHUNK_HEADS * HEAD_SIZE)
    keys = VISIBLE_KEYS + rows
    dma = pltpu.SemaphoreType.DMA
    return pl.pallas_call(
        functools.partial(kernel, n, q_width // width),
        out_shape=jax.ShapeDtypeStruct((rows, q_width), jnp.bfloat16),
        in_specs=[pl.BlockSpec(memory_space=pl.ANY)] * 4,
        out_specs=pl.BlockSpec(memory_space=pl.ANY),
        scratch_shapes=[
            pltpu.VMEM((2, keys, width), jnp.bfloat16),
            pltpu.VMEM((span + 1, 1, rows), jnp.int32),
            pltpu.VMEM((rows, q_width), jnp.bfloat16),
            pltpu.VMEM((rows, q_width), jnp.bfloat16),
            pltpu.VMEM((rows, keys), jnp.float32),
            dma((span, chunks)),
            dma((span + 1, chunks)),
            dma((span,)),
            dma((span + 1,)),
            dma((2, chunks)),
            dma,
            dma,
            dma((chunks,)),
        ],
        compiler_params=pltpu.CompilerParams(collective_id=0, has_side_effects=True),
    )(rotated_queries, rotated_keys, projected_values, doc_ids.reshape(1, rows))


def solution(mesh):
    in_specs = (P("ctx", "head"), P("ctx", "head"), P("ctx", "head"), P("ctx"))
    return jax.shard_map(
        functools.partial(per_device, mesh.shape["ctx"]),
        mesh=mesh,
        in_specs=in_specs,
        out_specs=P("ctx", "head"),
        check_vma=False,
    )
```

time: 223 us -> 70.1 us (0.31); the launches traced: 220 us -> 70 us
  starting transfers between devices: 138 us -> 0 us
  Pallas kernels: 0 us -> 67.7 us
  matrix products: 53.6 us -> 0 us
  local copies, waits for them, and re-layouts: 17.3 us -> 2.29 us
  other arithmetic: 9.95 us -> 0 us
    ppermute x24 -> x0, starting transfers between devices: 138 us -> none  [shifted(): lax.ppermute(value, axis, [(source, source + steps) for source in range(i...]
    pallas_call x0 -> x1, Pallas kernels: none -> 67.7 us  [per_device(): pl.pallas_call(functools.partial(kernel, n, q_width // width), out_shape=...]
    dot_general x18 -> x0, matrix products: 53.6 us -> none  [the longest x9 33.3 us: attend(): jnp.einsum('grtl,lgd->grtd', weights.astype(jnp.bfloat16), values.reshape...]
    ppermute x8 -> x0, local copies, waits for them, and re-layouts: 9.13 us -> none  [shifted(): lax.ppermute(value, axis, [(source, source + steps) for source in range(i...]
    reduce_sum x5 -> x0, other arithmetic: 7.05 us -> none  [attend(): total = total * fade + jnp.sum(weights, axis=-1)]
    reshape x2 -> x0, local copies, waits for them, and re-layouts: 3.84 us -> none  [the longest x1 2.05 us: attend(): values.reshape(length, kv_heads, HEAD_SIZE)]
  transfers between devices with their start and end apart: 24 -> 0, of which waited for: 0 -> 0; matrix products, arithmetic and copies ran while one was open for 31% -> 0% of each run, Pallas kernels for 0% -> 0%
where the time goes in v1:
time: 70.1 us; the launch traced here: 70 us
  Pallas kernels  67.7 us (97%)
  local copies, waits for them, and re-layouts  2.29 us (3%)
    pallas_call x1, Pallas kernels, per_device(): pl.pallas_call(functools.partial(kernel, n, q_width // width), out_shape=...  67.7 us
    unnamed x1, local copies, waits for them, and re-layouts  2.29 us

profile of v1, /device:TPU:0, one launch (start us, length us, event | category | flops | bytes accessed | tf_op | source)
XLA Modules:
  0.0 70.0 jit_solution(1808472405250421255)
XLA Ops:
  0.0 67.7 %shard_map.46 = bf16[128,4096]{1,0:T(8,128)(2,1)} custom-call(bf16[128,4096]{1,0:T(8,128)(2,1)} %q_hbm.1, bf16[128,2048]{1,0:T(8,128)(2,1)} %k_hbm.1, bf16[128,2048]{1,0:T(8,128)(2,1)} %v_hbm.1, s32[1,128]{1,0:T(1,128)} %bitcast.1), custom_call_target="tpu_custom_call" | custom-call | tf_op jit(solution)/shard_map/pallas_call | solution.py:262
  67.7 2.3 %copy.6 = bf16[128,4096]{1,0:T(8,128)(2,1)} copy(bf16[128,4096]{1,0:T(8,128)(2,1)} %shard_map.46) | data formatting | bytes 2097152

commit v2 on v1

--- a/solution.py
+++ b/solution.py
@@ -12,6 +12,7 @@
 VISIBLE_KEYS = 1024
 PRE_SCALAR = 168
 CHUNK_HEADS = 2
+AHEAD = 0
 MESH = pl.DeviceIdType.MESH
 
 
@@ -45,7 +46,6 @@
     cols = CHUNK_HEADS * HEAD_SIZE
     chunks = width // cols
     q_cols = cols * group
-    direct = chips
     me = lax.axis_index("ctx")
     local = lax.rem(me, span)
     base = me - local
@@ -58,12 +58,8 @@
     def back(dst, src):
         return lax.rem(dst - src + span, span)
 
-    def place(steps):
-        return pl.multiple_of((span - steps) * rows, rows)
-
     def block(steps, chunk):
-        start = pl.multiple_of(chunk * cols, cols)
-        return kv.at[:, pl.ds(place(steps), rows), pl.ds(start, cols)]
+        return kv.at[chunk, span - steps]
 
     def copy(src, dst, target, kind, chunk):
         return pltpu.make_async_remote_copy(
@@ -85,54 +81,100 @@
             device_id_type=MESH,
         )
 
-    def other(turn):
-        return lax.rem(chip + turn, chips)
+    beside = chip + 1 - 2 * lax.rem(chip, 2)
+    across = lax.rem(chip + 2, chips)
+    far = 3 - chip
+
+    def corner(source):
+        return lax.rem(source, 3) == 0
+
+    def by_across(source, chunk):
+        third = lax.rem(chunk, 3)
+        return jnp.logical_or(
+            jnp.logical_and(corner(source), third == 1),
+            jnp.logical_and(jnp.logical_not(corner(source)), third != 0),
+        )
+
+    def by_beside(source, chunk):
+        return jnp.logical_and(corner(source), jnp.logical_not(by_across(source, chunk)))
+
+    def straight(source, chunk):
+        return jnp.logical_not(jnp.logical_or(corner(source), by_across(source, chunk)))
+
+    def onward(copy, chunk):
+        copy(0, span, z_next, 0, chunk).start()
+
+    def send(copy, chunk, steps, chosen):
+        for kind, there in ((1, beside), (2, across), (3, far)):
+            to = 2 * there + core
+            wanted = chosen(to)
+            if kind == 3:
+                wanted = jnp.logical_and(wanted, straight(chip, chunk))
+
+            @pl.when(wanted)
+            def _():
+                copy(steps, back(to, local), base + to, kind, chunk).start()
+
+        @pl.when(chosen(sib))
+        def _():
+            copy(steps, back(sib, local), base + sib, 4, chunk).start()
 
     def send_own(copy, chunk):
-        copy(0, span, z_next, 0, chunk).start()
-        for turn in range(1, chips):
-            to = 2 * other(turn) + core
-
-            @pl.when(to > local)
-            def _():
-                copy(0, back(to, local), base + to, turn, chunk).start()
-
-        @pl.when(core == 0)
-        def _():
-            copy(0, back(sib, local), base + sib, direct, chunk).start()
+        send(copy, chunk, 0, lambda to: to > local)
 
     def send_past(copy, chunk):
         copy(0, span, z_next, 0, chunk).wait_recv()
-        for turn in range(1, chips):
-            to = 2 * other(turn) + core
-
-            @pl.when(to < local)
+        send(copy, chunk, span, lambda to: to < local)
+
+    def to_sib(copy, chunk, there, kind):
+        source = 2 * there + core
+        copy(back(local, source), back(sib, source), base + sib, kind, chunk).start()
+
+    def arrive(copy, chunk, there):
+        copy(0, back(local, 2 * there + core), z_next, 0, chunk).wait_recv()
+
+    def relay_near(copy, chunk):
+        for kind, there, target, chosen in (
+            (8, across, beside, by_across),
+            (9, beside, across, by_beside),
+        ):
+            arrive(copy, chunk, there)
+            source, to = 2 * there + core, 2 * target + core
+
+            @pl.when(chosen(there, chunk))
             def _():
-                copy(span, back(to, local), base + to, turn, chunk).start()
-
-        @pl.when(core == 1)
-        def _():
-            copy(span, back(sib, local), base + sib, direct, chunk).start()
-
-    def relay(copy, chunk):
-        for turn in range(1, chips):
-            source = 2 * other(turn) + core
-            here = back(local, source)
-            copy(0, here, z_next, 0, chunk).wait_recv()
-            copy(here, back(sib, source), base + sib, direct + turn, chunk).start()
+                copy(back(local, source), back(to, source), base + to, kind, chunk).start()
+
+            to_sib(copy, chunk, there, kind - 3)
+
+    def relay_far(copy, chunk):
+        arrive(copy, chunk, far)
+        to_sib(copy, chunk, far, 7)
 
     def gather(copy, chunk):
         copy(0, back(local, sib), z_next, 0, chunk).wait_recv()
-        for turn in range(1, chips):
-            source = 2 * other(turn) + 1 - core
-            copy(0, back(local, source), z_next, 0, chunk).wait_recv()
+        for there in (beside, across, far):
+            copy(0, back(local, 2 * there + 1 - core), z_next, 0, chunk).wait_recv()
+
+    def sent(copy, chunk):
+        for kind in (0, 1, 2, 4, 5, 6, 7):
+            copy(0, span, z_next, kind, chunk).wait_send()
+        for kind, wanted in (
+            (3, straight(chip, chunk)),
+            (8, by_across(across, chunk)),
+            (9, by_beside(beside, chunk)),
+        ):
+
+            @pl.when(wanted)
+            def _():
+                copy(0, span, z_next, kind, chunk).wait_send()
 
     def own_copies(chunk):
         start = pl.multiple_of(chunk * cols, cols)
         return [
             pltpu.make_async_copy(
                 ref.at[:, pl.ds(start, cols)],
-                kv.at[which, pl.ds(VISIBLE_KEYS, rows), pl.ds(start, cols)],
+                kv.at[chunk, span, which],
                 own_sem.at[which, chunk],
             )
             for which, ref in enumerate((k_hbm, v_hbm))
@@ -157,28 +199,41 @@
 
     barrier = pltpu.get_barrier_semaphore()
     partners = [z_next, z_prev, base + sib] + [
-        base + 2 * other(turn) + core for turn in range(1, chips)
+        base + 2 * there + core for there in (beside, across, far)
     ]
     for partner in partners:
         pl.semaphore_signal(barrier, inc=1, device_id={"ctx": partner}, device_id_type=MESH)
     pl.semaphore_wait(barrier, len(partners))
 
     own_ids.wait()
-    send_own(ids_copy, 0)
+    onward(ids_copy, 0)
 
     def start_own(chunk, _):
         for c in own_copies(chunk):
             c.wait()
+        onward(copy, chunk)
+        return 0
+
+    lax.fori_loop(0, 1, start_own, 0)
+    send_own(ids_copy, 0)
+    send_own(copy, 0)
+    lax.fori_loop(1, min(AHEAD + 4, chunks), start_own, 0)
+
+    def ahead(chunk, _):
         send_own(copy, chunk)
         return 0
 
-    lax.fori_loop(0, chunks, start_own, 0)
+    lax.fori_loop(1, min(AHEAD + 3, chunks), ahead, 0)
 
     send_past(ids_copy, 0)
     send_past(copy, 0)
-    relay(ids_copy, 0)
+    relay_near(ids_copy, 0)
     send_past(copy, 1)
-    relay(copy, 0)
+    relay_near(copy, 0)
+    relay_far(ids_copy, 0)
+    send_past(copy, 2)
+    relay_near(copy, 1)
+    relay_far(copy, 0)
     gather(ids_copy, 0)
 
     own_row = ids[0].astype(jnp.float32)
@@ -198,19 +253,27 @@
     factor = PRE_SCALAR ** (-0.5) * math.log2(math.e)
 
     def step(chunk, _):
-        @pl.when(chunk + 2 < chunks)
+        @pl.when(chunk + AHEAD + 4 < chunks)
         def _():
-            send_past(copy, chunk + 2)
-
-        @pl.when(chunk + 1 < chunks)
-        def _():
-            relay(copy, chunk + 1)
+            start_own(chunk + AHEAD + 4, 0)
+
+        for later, act in (
+            (3 + AHEAD, send_own),
+            (3, send_past),
+            (2, relay_near),
+            (1, relay_far),
+        ):
+
+            @pl.when(chunk + later < chunks)
+            def _():
+                act(copy, chunk + later)
 
         gather(copy, chunk)
         for head in range(CHUNK_HEADS):
             at = pl.multiple_of(chunk * cols + head * HEAD_SIZE, HEAD_SIZE)
-            key_rows = kv[0, :, pl.ds(at, HEAD_SIZE)]
-            values = kv[1, :, pl.ds(at, HEAD_SIZE)]
+            lanes = slice(head * HEAD_SIZE, (head + 1) * HEAD_SIZE)
+            key_rows = kv[chunk, :, 0, :, lanes].reshape(keys, HEAD_SIZE)
+            values = kv[chunk, :, 1, :, lanes].reshape(keys, HEAD_SIZE)
             weights, totals = [], []
             queries = jnp.concatenate(
                 [
@@ -242,14 +305,12 @@
     lax.fori_loop(0, chunks, step, 0)
 
     def finish(chunk, _):
-        for kind in range(2 * chips):
-            copy(0, span, z_next, kind, chunk).wait_send()
+        sent(copy, chunk)
         out_copy(chunk).wait()
         return 0
 
     lax.fori_loop(0, chunks, finish, 0)
-    for kind in range(2 * chips):
-        ids_copy(0, span, z_next, kind, 0).wait_send()
+    sent(ids_copy, 0)
 
 
 def per_device(n, rotated_queries, rotated_keys, projected_values, doc_ids):
@@ -265,14 +326,14 @@
         in_specs=[pl.BlockSpec(memory_space=pl.ANY)] * 4,
         out_specs=pl.BlockSpec(memory_space=pl.ANY),
         scratch_shapes=[
-            pltpu.VMEM((2, keys, width), jnp.bfloat16),
+            pltpu.VMEM((chunks, span + 1, 2, rows, width // chunks), jnp.bfloat16),
             pltpu.VMEM((span + 1, 1, rows), jnp.int32),
             pltpu.VMEM((rows, q_width), jnp.bfloat16),
             pltpu.VMEM((rows, q_width), jnp.bfloat16),
             pltpu.VMEM((rows, keys), jnp.float32),
-            dma((span, chunks)),
+            dma((10, chunks)),
             dma((span + 1, chunks)),
-            dma((span,)),
+            dma((10,)),
             dma((span + 1,)),
             dma((2, chunks)),
             dma,

time: 70.1 us -> 59 us (0.84)
  Pallas kernels: 67.7 us -> 56.5 us
    pallas_call x1, Pallas kernels: 67.7 us -> 56.5 us  [per_device(): pl.pallas_call(functools.partial(kernel, n, q_width // width), out_shape=...]
where the time goes in v2:
time: 59 us; the launch traced here: 58.8 us
  Pallas kernels  56.5 us (96%)
  local copies, waits for them, and re-layouts  2.29 us (4%)
    pallas_call x1, Pallas kernels, per_device(): pl.pallas_call(functools.partial(kernel, n, q_width // width), out_shape=...  56.5 us
    unnamed x1, local copies, waits for them, and re-layouts  2.29 us

profile of v2, /device:TPU:0, one launch (start us, length us, event | category | flops | bytes accessed | tf_op | source)
XLA Modules:
  0.0 58.8 jit_solution(9058588825644087035)
XLA Ops:
  0.0 56.5 %shard_map.46 = bf16[128,4096]{1,0:T(8,128)(2,1)} custom-call(bf16[128,4096]{1,0:T(8,128)(2,1)} %q_hbm.1, bf16[128,2048]{1,0:T(8,128)(2,1)} %k_hbm.1, bf16[128,2048]{1,0:T(8,128)(2,1)} %v_hbm.1, s32[1,128]{1,0:T(1,128)} %bitcast.1), custom_call_target="tpu_custom_call" | custom-call | tf_op jit(solution)/shard_map/pallas_call | solution.py:323
  56.5 2.3 %copy.6 = bf16[128,4096]{1,0:T(8,128)(2,1)} copy(bf16[128,4096]{1,0:T(8,128)(2,1)} %shard_map.46) | data formatting | bytes 2097152

commit v3 on v2

--- a/solution.py
+++ b/solution.py
@@ -11,8 +11,11 @@
 HEAD_SIZE = 128
 VISIBLE_KEYS = 1024
 PRE_SCALAR = 168
-CHUNK_HEADS = 2
+CHUNK_HEADS = 1
 AHEAD = 0
+PAST = 6
+NEAR = 4
+FAR = 2
 MESH = pl.DeviceIdType.MESH
 
 
@@ -37,6 +40,8 @@
     q_sem,
     ids_sem,
     out_sem,
+    stand_sem,
+    ids_stand_sem,
 ):
     rows = q_hbm.shape[0]
     width = k_hbm.shape[1]
@@ -101,8 +106,31 @@
     def straight(source, chunk):
         return jnp.logical_not(jnp.logical_or(corner(source), by_across(source, chunk)))
 
+    def stand_in(chunk):
+        start = pl.multiple_of(chunk * cols, cols)
+        return [
+            pltpu.make_async_copy(
+                ref.at[:, pl.ds(start, cols)], kv.at[chunk, 0, which], stand_sem.at[which, chunk]
+            )
+            for which, ref in enumerate((k_hbm, v_hbm))
+        ]
+
+    ids_stand = pltpu.make_async_copy(ids_hbm, ids.at[span], ids_stand_sem)
+
     def onward(copy, chunk):
-        copy(0, span, z_next, 0, chunk).start()
+        @pl.when(me + span < n)
+        def _():
+            copy(0, span, z_next, 0, chunk).start()
+
+    def past_here(copy, chunk):
+        @pl.when(me >= span)
+        def _():
+            copy(0, span, z_next, 0, chunk).wait_recv()
+
+        @pl.when(me < span)
+        def _():
+            for c in [ids_stand] if copy is ids_copy else stand_in(chunk):
+                c.wait()
 
     def send(copy, chunk, steps, chosen):
         for kind, there in ((1, beside), (2, across), (3, far)):
@@ -123,7 +151,7 @@
         send(copy, chunk, 0, lambda to: to > local)
 
     def send_past(copy, chunk):
-        copy(0, span, z_next, 0, chunk).wait_recv()
+        past_here(copy, chunk)
         send(copy, chunk, span, lambda to: to < local)
 
     def to_sib(copy, chunk, there, kind):
@@ -157,9 +185,10 @@
             copy(0, back(local, 2 * there + 1 - core), z_next, 0, chunk).wait_recv()
 
     def sent(copy, chunk):
-        for kind in (0, 1, 2, 4, 5, 6, 7):
+        for kind in (1, 2, 4, 5, 6, 7):
             copy(0, span, z_next, kind, chunk).wait_send()
         for kind, wanted in (
+            (0, me + span < n),
             (3, straight(chip, chunk)),
             (8, by_across(across, chunk)),
             (9, by_beside(beside, chunk)),
@@ -189,9 +218,19 @@
 
     own_ids.start()
 
+    @pl.when(me < span)
+    def _():
+        ids_stand.start()
+
     def fetch(chunk, _):
         for c in own_copies(chunk):
             c.start()
+
+        @pl.when(me < span)
+        def _():
+            for c in stand_in(chunk):
+                c.start()
+
         return 0
 
     lax.fori_loop(0, chunks, fetch, 0)
@@ -217,23 +256,24 @@
     lax.fori_loop(0, 1, start_own, 0)
     send_own(ids_copy, 0)
     send_own(copy, 0)
-    lax.fori_loop(1, min(AHEAD + 4, chunks), start_own, 0)
+    lax.fori_loop(1, min(AHEAD + PAST + 1, chunks), start_own, 0)
 
     def ahead(chunk, _):
         send_own(copy, chunk)
         return 0
 
-    lax.fori_loop(1, min(AHEAD + 3, chunks), ahead, 0)
-
-    send_past(ids_copy, 0)
-    send_past(copy, 0)
-    relay_near(ids_copy, 0)
-    send_past(copy, 1)
-    relay_near(copy, 0)
-    relay_far(ids_copy, 0)
-    send_past(copy, 2)
-    relay_near(copy, 1)
-    relay_far(copy, 0)
+    lax.fori_loop(1, min(AHEAD + PAST, chunks), ahead, 0)
+
+    def first(act, chunk):
+        if chunk == 0:
+            act(ids_copy, 0)
+        if 0 <= chunk < chunks:
+            act(copy, chunk)
+
+    for turn in range(-PAST, 0):
+        first(send_past, turn + PAST)
+        first(relay_near, turn + NEAR)
+        first(relay_far, turn + FAR)
     gather(ids_copy, 0)
 
     own_row = ids[0].astype(jnp.float32)
@@ -253,15 +293,14 @@
     factor = PRE_SCALAR ** (-0.5) * math.log2(math.e)
 
     def step(chunk, _):
-        @pl.when(chunk + AHEAD + 4 < chunks)
-        def _():
-            start_own(chunk + AHEAD + 4, 0)
+        @pl.when(chunk + AHEAD + PAST + 1 < chunks)
+        def _():
+            start_own(chunk + AHEAD + PAST + 1, 0)
 
         for later, act in (
-            (3 + AHEAD, send_own),
-            (3, send_past),
-            (2, relay_near),
-            (1, relay_far),
+            (PAST + AHEAD, send_own),
+            (PAST, send_past),
+            (NEAR, relay_near),
         ):
 
             @pl.when(chunk + later < chunks)
@@ -300,6 +339,11 @@
                     summed[g * rows : (g + 1) * rows] / totals[g]
                 ).astype(jnp.bfloat16)
         out_copy(chunk).start()
+
+        @pl.when(chunk + FAR < chunks)
+        def _():
+            relay_far(copy, chunk + FAR)
+
         return 0
 
     lax.fori_loop(0, chunks, step, 0)
@@ -339,6 +383,8 @@
             dma,
             dma,
             dma((chunks,)),
+            dma((2, chunks)),
+            dma,
         ],
         compiler_params=pltpu.CompilerParams(collective_id=0, has_side_effects=True),
     )(rotated_queries, rotated_keys, projected_values, doc_ids.reshape(1, rows))

time: 59 us -> 57.5 us (0.975)
  Pallas kernels: 56.5 us -> 54.6 us
    pallas_call x1, Pallas kernels: 56.5 us -> 54.6 us  [per_device(): pl.pallas_call(functools.partial(kernel, n, q_width // width), out_shape=...]
where the time goes in v3:
time: 57.5 us; the launch traced here: 56.9 us
  Pallas kernels  54.6 us (95%)
  local copies, waits for them, and re-layouts  2.29 us (4%)
    pallas_call x1, Pallas kernels, per_device(): pl.pallas_call(functools.partial(kernel, n, q_width // width), out_shape=...  54.6 us
    unnamed x1, local copies, waits for them, and re-layouts  2.29 us

profile of v3, /device:TPU:0, one launch (start us, length us, event | category | flops | bytes accessed | tf_op | source)
XLA Modules:
  0.0 56.9 jit_solution(700604728301584367)
XLA Ops:
  0.0 54.6 %shard_map.46 = bf16[128,4096]{1,0:T(8,128)(2,1)} custom-call(bf16[128,4096]{1,0:T(8,128)(2,1)} %q_hbm.1, bf16[128,2048]{1,0:T(8,128)(2,1)} %k_hbm.1, bf16[128,2048]{1,0:T(8,128)(2,1)} %v_hbm.1, s32[1,128]{1,0:T(1,128)} %bitcast.1), custom_call_target="tpu_custom_call" | custom-call | tf_op jit(solution)/shard_map/pallas_call | solution.py:367
  54.6 2.3 %copy.6 = bf16[128,4096]{1,0:T(8,128)(2,1)} copy(bf16[128,4096]{1,0:T(8,128)(2,1)} %shard_map.46) | data formatting | bytes 2097152

commit v4 on v3

--- a/solution.py
+++ b/solution.py
@@ -13,7 +13,7 @@
 PRE_SCALAR = 168
 CHUNK_HEADS = 1
 AHEAD = 0
-PAST = 6
+PAST = 7
 NEAR = 4
 FAR = 2
 MESH = pl.DeviceIdType.MESH

time: 57.5 us -> 57 us (level)
  no operation moved by 1% of the time
where the time goes in v4:
time: 57 us; the launch traced here: 56.4 us
  Pallas kernels  54.1 us (95%)
  local copies, waits for them, and re-layouts  2.29 us (4%)
    pallas_call x1, Pallas kernels, per_device(): pl.pallas_call(functools.partial(kernel, n, q_width // width), out_shape=...  54.1 us
    unnamed x1, local copies, waits for them, and re-layouts  2.29 us

profile of v4, /device:TPU:0, one launch (start us, length us, event | category | flops | bytes accessed | tf_op | source)
XLA Modules:
  0.0 56.4 jit_solution(1964917733827600802)
XLA Ops:
  0.0 54.1 %shard_map.46 = bf16[128,4096]{1,0:T(8,128)(2,1)} custom-call(bf16[128,4096]{1,0:T(8,128)(2,1)} %q_hbm.1, bf16[128,2048]{1,0:T(8,128)(2,1)} %k_hbm.1, bf16[128,2048]{1,0:T(8,128)(2,1)} %v_hbm.1, s32[1,128]{1,0:T(1,128)} %bitcast.1), custom_call_target="tpu_custom_call" | custom-call | tf_op jit(solution)/shard_map/pallas_call | solution.py:367
  54.2 2.3 %copy.6 = bf16[128,4096]{1,0:T(8,128)(2,1)} copy(bf16[128,4096]{1,0:T(8,128)(2,1)} %shard_map.46) | data formatting | bytes 2097152
